TPU v7x, 256 devices: a whole 4x4x8 slice. The times are simulated.
256 devices in a mesh: worker: 16 (over x, z_hi, core), fsdp: 16 (over z_lo, y).
Axes of the slice: x: 4, y: 4, z: 8 (z_hi: 2, z_lo: 4; z = z_hi * 4 + z_lo), core: 2. Of those that a mesh axis runs over, the one named last changes fastest.
Arguments:
- inputs: bfloat16 [16, 4096, 8192], P('worker', 'fsdp'), may hold values from -6 to 6
- output_grads: bfloat16 [16, 4096, 1024], P('worker', 'fsdp'), may hold values from -0.25 to 0.25
- local_params: float32 [16, 8192, 1024], P('worker', 'fsdp'), may hold values from -6 to 6
- first_moment: float32 [16, 8192, 1024], P('worker', 'fsdp'), may hold values from -4 to 4
- second_moment: float32 [16, 8192, 1024], P('worker', 'fsdp'), may hold values from 0.01 to 0.1
- global_params: float32 [8192, 1024], P(('fsdp', 'worker')), may hold values from -6 to 6
- momentum: float32 [8192, 1024], P(('fsdp', 'worker')), may hold values from -6 to 6
Outputs:
- new_params: float32 [8192, 1024], P('fsdp')
- new_momentum: float32 [8192, 1024], P(('fsdp', 'worker'))
All inputs are finite; a program needn't handle non-finite values.
Results may differ from a plain program's by a relative error of at most 0.0015.
Values may be sent and summed in bfloat16 or wider, within the bound.
A program may use at most 128 MiB of HBM per device.

v0:
```python
import jax
import jax.numpy as jnp
from jax import lax
from jax.sharding import PartitionSpec as P

beta_first = 0.8
beta_second = 0.9
inner_rate = 0.15
weight_decay = 0.1
adam_epsilon = 1e-08
outer_rate = 0.7
momentum_coef = 0.9
inner_count = 50


def shards(
    inputs, output_grads, local_params, first_moment, second_moment, global_params, momentum
):
    features = inputs[0]
    cotangents = output_grads[0]
    params = local_params[0]
    gradient = lax.psum_scatter(
        lax.dot_general(
            features, cotangents, (((0,), (0,)), ((), ())), preferred_element_type=jnp.float32
        ).astype(jnp.bfloat16),
        "fsdp",
        scatter_dimension=0,
        tiled=True,
    ).astype(jnp.float32)
    moment_one = beta_first * first_moment[0] + (1.0 - beta_first) * gradient
    moment_two = beta_second * second_moment[0] + (1.0 - beta_second) * gradient * gradient
    first_correction = 1.0 - beta_first**inner_count
    second_correction = 1.0 - beta_second**inner_count
    ratio = (
        moment_one / first_correction / (jnp.sqrt(moment_two / second_correction) + adam_epsilon)
    )
    stepped = params - inner_rate * (ratio + weight_decay * params)
    replicas = lax.axis_size("worker")
    anchor, moment_rows = (
        lax.all_gather(global_params, "worker", axis=0, tiled=True),
        lax.all_gather(momentum, "worker", axis=0, tiled=True),
    )
    pseudo_grad = anchor - stepped
    outer_grad = lax.psum(pseudo_grad, "worker") / replicas
    moment_full = momentum_coef * moment_rows + outer_grad
    fresh_rows = anchor - outer_rate * (outer_grad + momentum_coef * moment_full)
    share_rows = global_params.shape[0]
    worker_index = lax.axis_index("worker")
    own_moment = lax.dynamic_slice_in_dim(moment_full, worker_index * share_rows, share_rows, 0)
    return (fresh_rows, own_moment)


def solution(mesh):
    return jax.shard_map(
        shards,
        mesh=mesh,
        in_specs=(
            P("worker", "fsdp", None),
            P("worker", "fsdp", None),
            P("worker", "fsdp", None),
            P("worker", "fsdp", None),
            P("worker", "fsdp", None),
            P(("fsdp", "worker"), None),
            P(("fsdp", "worker"), None),
        ),
        out_specs=(P("fsdp", None), P(("fsdp", "worker"), None)),
        check_vma=False,
    )
```

profile of v0, /device:TPU:24, one launch (start us, length us, event | category | flops | bytes accessed | tf_op | source)
XLA Modules:
  0.0 505.8 jit_solution(11412425260126326226)
XLA Ops:
  8.0 0.0 copy-start
  8.0 0.0 all-gather.3.cloned.1.call-start
  8.1 0.7 all-gather.3.cloned.1.call-update
  8.7 0.0 reduce-scatter.2.cloned.1.call-start
  8.8 0.2 copy-done
  9.0 10.5 %convolution_convert_fusion = bf16[8192,1024]{1,0:T(8,128)(2,1)} fusion(bf16[1,256,8192]{2,1,0:T(8,128)(2,1)} %param.7, bf16[1,256,1024]{2,1,0:T(8,128)(2,1)S(1)} %copy-done), kind=kOutput, calls=%fused_computation | convolution fusion | flops 4303355904 | bytes 21495808 | tf_op jit(solution)/shard_map/dot_general | solution.py:23
  19.5 0.0 copy-start.2
  19.5 0.0 reduce-scatter.2.cloned.1.call-update
  19.5 0.0 all-gather.5.cloned.1.call-start
  19.6 0.7 all-gather.5.cloned.1.call-update
  20.3 0.0 all-reduce.2.cloned.1.call-start
  20.3 65.4 %all-gather.3.cloned.1.call-done = f32[512,1024]{1,0:T(8,128)} async-done(((f32[32,1024]{1,0:T(8,128)}), f32[512,1024]{1,0:T(8,128)}) %all-gather.3.cloned.1.call-update) | async-done | bytes 2097168 | tf_op jit(solution)/shard_map/all_gather | solution.py:40
  85.7 130.7 %reduce-scatter.2.cloned.1.call-done = bf16[512,1024]{1,0:T(8,128)(2,1)} async-done(((bf16[8192,1024]{1,0:T(8,128)(2,1)}), bf16[512,1024]{1,0:T(8,128)(2,1)}) %reduce-scatter.2.cloned.1.call-update) | async-done | bytes 1048592 | tf_op jit(solution)/shard_map/reduce_scatter | solution.py:22
  216.4 0.0 copy-done.2
  216.4 6.2 %fusion.7 = f32[512,1024]{1,0:T(8,128)} fusion(f32[512,1024]{1,0:T(8,128)} %all-gather.3.cloned.1.call-done, bf16[512,1024]{1,0:T(8,128)(2,1)} %reduce-scatter.2.cloned.1.call-done, f32[1,512,1024]{2,1,0:T(8,128)S(1)} %copy-done.2, f32[1,512,1024]{2,1,0:T(8,128)} %param.11, f32[1,512,1024]{2,1,0:T(8,128)} %param.10), kind=kLoop, calls=%fused_computation.10 | loop fusion | flops 8912896 | bytes 11534336 | tf_op jit(solution)/shard_map/sub | solution.py:43
  222.6 0.0 copy-start.1
  222.7 0.0 all-reduce.2.cloned.1.call-update
  222.7 68.5 %all-gather.5.cloned.1.call-done = f32[512,1024]{1,0:T(8,128)} async-done(((f32[32,1024]{1,0:T(8,128)}), f32[512,1024]{1,0:T(8,128)}) %all-gather.5.cloned.1.call-update) | async-done | bytes 2097168 | tf_op jit(solution)/shard_map/all_gather | solution.py:41
  291.2 202.5 %all-reduce.2.cloned.1.call-done = f32[512,1024]{1,0:T(8,128)} async-done(((f32[512,1024]{1,0:T(8,128)}), f32[512,1024]{1,0:T(8,128)}) %all-reduce.2.cloned.1.call-update) | async-done | bytes 2097168 | tf_op jit(solution)/shard_map/psum | solution.py:44
  493.7 0.0 copy-done.1
  493.7 4.3 multiply_add_fusion
  498.0 0.7 constant_dynamic-slice_fusion
Async XLA Ops:
  8.0 1.0 copy-start
  8.0 77.7 %all-gather.3.cloned.1.call-start = ((), (), s32[]{:S(2)}) async-start(), calls=%async_computation.1 | async-start | bytes 2228224 | tf_op jit(solution)/shard_map/all_gather | solution.py:40
  8.7 207.7 %reduce-scatter.2.cloned.1.call-start = ((), (), s32[]{:S(2)}) async-start(), calls=%async_computation.2 | async-start | bytes 17825792 | tf_op jit(solution)/shard_map/reduce_scatter | solution.py:22
  19.5 196.9 %copy-start.2 = (f32[1,512,1024]{2,1,0:T(8,128)S(1)}, f32[1,512,1024]{2,1,0:T(8,128)}, u32[]{:S(2)}) copy-start(f32[1,512,1024]{2,1,0:T(8,128)} %param.9) | copy-start | bytes 6291460
  19.5 271.6 %all-gather.5.cloned.1.call-start = ((), (), s32[]{:S(2)}) async-start(), calls=%async_computation.4 | async-start | bytes 2228224 | tf_op jit(solution)/shard_map/all_gather | solution.py:41
  20.3 473.4 %all-reduce.2.cloned.1.call-start = ((), (), s32[]{:S(2)}) async-start(), calls=%async_computation.3 | async-start | bytes 4194304 | tf_op jit(solution)/shard_map/psum | solution.py:44
  222.6 271.1 %copy-start.1 = (f32[512,1024]{1,0:T(8,128)S(1)}, f32[512,1024]{1,0:T(8,128)}, u32[]{:S(2)}) copy-start(f32[512,1024]{1,0:T(8,128)} %all-gather.3.cloned.1.call-done) | copy-start | bytes 6291460
Sparse Core Ops, SparseCore 0:
  11.5 74.1 all-gather.2
  88.4 202.7 all-gather.4
  294.4 199.2 all-reduce.1
Sparse Core Ops, SparseCore 1:
  19.6 196.8 reduce-scatter.1
where the time goes:
time: 506 us
  waiting for transfers between devices  469 us (93%)
  between operations  15.2 us (3%)
  matrix products  10.5 us (2%)
  other arithmetic  10.5 us (2%)
    psum x1, waiting for transfers between devices, shards(): outer_grad = lax.psum(pseudo_grad, 'worker') / replicas  203 us
    reduce_scatter x1, waiting for transfers between devices, shards(): lax.psum_scatter(lax.dot_general(features, cotangents, (((0,), (0,)), (()...  131 us
    all_gather x1, waiting for transfers between devices, shards(): lax.all_gather(momentum, 'worker', axis=0, tiled=True)  68.5 us
    all_gather x1, waiting for transfers between devices, shards(): lax.all_gather(global_params, 'worker', axis=0, tiled=True)  65.4 us
    dot_general x1, matrix products, shards(): lax.dot_general(features, cotangents, (((0,), (0,)), ((), ())), preferred...  10.5 us
  transfers between devices with their start and end apart: 4, of which 4 were waited for; matrix products, arithmetic and copies ran while one was open for 3% of the time, Pallas kernels for 0%

commit v1 on v0

--- a/solution.py
+++ b/solution.py
@@ -41,7 +41,7 @@
         lax.all_gather(momentum, "worker", axis=0, tiled=True),
     )
     pseudo_grad = anchor - stepped
-    outer_grad = lax.psum(pseudo_grad, "worker") / replicas
+    outer_grad = jnp.sum(lax.all_gather(pseudo_grad, "worker"), axis=0) / replicas
     moment_full = momentum_coef * moment_rows + outer_grad
     fresh_rows = anchor - outer_rate * (outer_grad + momentum_coef * moment_full)
     share_rows = global_params.shape[0]

time: 506 us -> 615 us (1.22)
  waiting for transfers between devices: 469 us -> 564 us
  other arithmetic: 10.5 us -> 22.7 us
    all_gather x0 -> x1, waiting for transfers between devices: none -> 318 us  [shards(): lax.all_gather(pseudo_grad, 'worker')]
    psum x1 -> x0, waiting for transfers between devices: 203 us -> none  [shards(): outer_grad = lax.psum(pseudo_grad, 'worker') / replicas]
    all_gather x1, waiting for transfers between devices: 68.5 us -> 47.8 us  [shards(): lax.all_gather(momentum, 'worker', axis=0, tiled=True)]
    reduce_sum x0 -> x1, other arithmetic: none -> 12.1 us  [shards(): jnp.sum(lax.all_gather(pseudo_grad, 'worker'), axis=0) / replicas]
  transfers between devices with their start and end apart: 4 -> 4, of which waited for: 4 -> 4; matrix products, arithmetic and copies ran while one was open for 3% -> 4% of each run, Pallas kernels for 0% -> 0%
where the time goes in v1:
time: 615 us; the launch traced here: 613 us
  waiting for transfers between devices  564 us (92%)
  other arithmetic  22.7 us (4%)
  between operations  15.2 us (2%)
  matrix products  10.5 us (2%)
    all_gather x1, waiting for transfers between devices, shards(): lax.all_gather(pseudo_grad, 'worker')  318 us
    reduce_scatter x1, waiting for transfers between devices, shards(): lax.psum_scatter(lax.dot_general(features, cotangents, (((0,), (0,)), (()...  131 us
    all_gather x1, waiting for transfers between devices, shards(): lax.all_gather(global_params, 'worker', axis=0, tiled=True)  66.1 us
    all_gather x1, waiting for transfers between devices, shards(): lax.all_gather(momentum, 'worker', axis=0, tiled=True)  47.8 us
  transfers between devices with their start and end apart: 4, of which 4 were waited for; matrix products, arithmetic and copies ran while one was open for 4% of the time, Pallas kernels for 0%

profile of v1, /device:TPU:24, one launch (start us, length us, event | category | flops | bytes accessed | tf_op | source)
XLA Modules:
  0.0 613.0 jit_solution(11072957836683714489)
XLA Ops:
  8.0 0.0 copy-start
  8.0 0.0 all-gather.5.cloned.1.call-start
  8.1 0.7 all-gather.5.cloned.1.call-update
  8.7 0.0 reduce-scatter.2.cloned.1.call-start
  8.8 0.2 copy-done
  9.0 10.5 %convolution_convert_fusion = bf16[8192,1024]{1,0:T(8,128)(2,1)} fusion(bf16[1,256,8192]{2,1,0:T(8,128)(2,1)} %param.7, bf16[1,256,1024]{2,1,0:T(8,128)(2,1)S(1)} %copy-done), kind=kOutput, calls=%fused_computation | convolution fusion | flops 4303355904 | bytes 21495808 | tf_op jit(solution)/shard_map/dot_general | solution.py:23
  19.5 0.0 copy-start.2
  19.5 0.0 reduce-scatter.2.cloned.1.call-update
  19.5 0.0 all-gather.9.cloned.1.call-start
  19.6 66.1 %all-gather.5.cloned.1.call-done = f32[512,1024]{1,0:T(8,128)} async-done(((f32[32,1024]{1,0:T(8,128)}), f32[512,1024]{1,0:T(8,128)}) %all-gather.5.cloned.1.call-update) | async-done | bytes 2097168 | tf_op jit(solution)/shard_map/all_gather | solution.py:40
  85.7 130.7 %reduce-scatter.2.cloned.1.call-done = bf16[512,1024]{1,0:T(8,128)(2,1)} async-done(((bf16[8192,1024]{1,0:T(8,128)(2,1)}), bf16[512,1024]{1,0:T(8,128)(2,1)}) %reduce-scatter.2.cloned.1.call-update) | async-done | bytes 1048592 | tf_op jit(solution)/shard_map/reduce_scatter | solution.py:22
  216.4 0.0 copy-done.2
  216.4 6.2 %fusion.7 = f32[512,1024]{1,0:T(8,128)} fusion(f32[512,1024]{1,0:T(8,128)} %all-gather.5.cloned.1.call-done, bf16[512,1024]{1,0:T(8,128)(2,1)} %reduce-scatter.2.cloned.1.call-done, f32[1,512,1024]{2,1,0:T(8,128)S(1)} %copy-done.2, f32[1,512,1024]{2,1,0:T(8,128)} %param.11, f32[1,512,1024]{2,1,0:T(8,128)} %param.10), kind=kLoop, calls=%fused_computation.10 | loop fusion | flops 8912896 | bytes 11534336 | tf_op jit(solution)/shard_map/sub | solution.py:43
  222.7 0.0 all-gather.9.cloned.1.call-update
  222.7 0.0 all-gather.7.cloned.1.call-start
  222.7 0.7 all-gather.7.cloned.1.call-update
  223.4 317.5 %all-gather.9.cloned.1.call-done = f32[8192,1024]{1,0:T(8,128)} async-done(((f32[512,1024]{1,0:T(8,128)}), f32[8192,1024]{1,0:T(8,128)}) %all-gather.9.cloned.1.call-update) | async-done | bytes 33554448 | tf_op jit(solution)/shard_map/all_gather | solution.py:44
  541.0 12.1 %reduce_sum.9 = f32[512,1024]{1,0:T(8,128)S(1)} reduce(f32[16,512,1024]{2,1,0:T(8,128)} %bitcast.16, f32[]{:T(128)} %constant.13.clone.1), dimensions={0}, to_apply=%region_1.0 | reduce | flops 7864320 | bytes 35651588 | tf_op jit(solution)/shard_map/reduce_sum | solution.py:44
  553.1 47.8 %all-gather.7.cloned.1.call-done = f32[512,1024]{1,0:T(8,128)} async-done(((f32[32,1024]{1,0:T(8,128)}), f32[512,1024]{1,0:T(8,128)}) %all-gather.7.cloned.1.call-update) | async-done | bytes 2097168 | tf_op jit(solution)/shard_map/all_gather | solution.py:41
  600.9 0.0 copy-start.1
  600.9 4.4 multiply_add_fusion
  605.2 0.7 constant_dynamic-slice_fusion
  605.9 0.0 copy-done.1
Async XLA Ops:
  8.0 1.1 copy-start
  8.0 77.7 %all-gather.5.cloned.1.call-start = ((), (), s32[]{:S(2)}) async-start(), calls=%async_computation.1 | async-start | bytes 2228224 | tf_op jit(solution)/shard_map/all_gather | solution.py:40
  8.7 207.7 %reduce-scatter.2.cloned.1.call-start = ((), (), s32[]{:S(2)}) async-start(), calls=%async_computation.2 | async-start | bytes 17825792 | tf_op jit(solution)/shard_map/reduce_scatter | solution.py:22
  19.5 196.9 %copy-start.2 = (f32[1,512,1024]{2,1,0:T(8,128)S(1)}, f32[1,512,1024]{2,1,0:T(8,128)}, u32[]{:S(2)}) copy-start(f32[1,512,1024]{2,1,0:T(8,128)} %param.9) | copy-start | bytes 6291460
  19.5 521.4 %all-gather.9.cloned.1.call-start = ((), (), s32[]{:S(2)}) async-start(), calls=%async_computation.4 | async-start | bytes 35651584 | tf_op jit(solution)/shard_map/all_gather | solution.py:44
  222.7 378.2 %all-gather.7.cloned.1.call-start = ((), (), s32[]{:S(2)}) async-start(), calls=%async_computation.3 | async-start | bytes 2228224 | tf_op jit(solution)/shard_map/all_gather | solution.py:41
  600.9 5.0 copy-start.1
Sparse Core Ops, SparseCore 0:
  11.5 74.1 all-gather.4
  222.8 318.1 all-gather.8
  543.7 57.1 all-gather.6
Sparse Core Ops, SparseCore 1:
  19.6 196.8 reduce-scatter.1

commit v2 on v0

--- a/solution.py
+++ b/solution.py
@@ -37,7 +37,10 @@
     stepped = params - inner_rate * (ratio + weight_decay * params)
     replicas = lax.axis_size("worker")
     anchor, moment_rows = (
-        lax.all_gather(global_params, "worker", axis=0, tiled=True),
+        jnp.concatenate(
+            lax.all_to_all(jnp.stack([global_params] * lax.axis_size("worker")), "worker", 0, 0),
+            axis=0,
+        ),
         lax.all_gather(momentum, "worker", axis=0, tiled=True),
     )
     pseudo_grad = anchor - stepped

time: 506 us -> 487 us (0.962)
  waiting for transfers between devices: 469 us -> 434 us
  starting transfers between devices: 0.16 us -> 11.2 us
    all_to_all x0 -> x1, waiting for transfers between devices: none -> 76.6 us  [shards(): lax.all_to_all(jnp.stack([global_params] * lax.axis_size('worker')), 'wor...]
    all_gather x1, waiting for transfers between devices: 68.5 us -> 0.03 us  [shards(): lax.all_gather(momentum, 'worker', axis=0, tiled=True)]
    all_gather x1 -> x0, waiting for transfers between devices: 65.4 us -> none  [shards(): lax.all_gather(global_params, 'worker', axis=0, tiled=True)]
    reduce_scatter x1, waiting for transfers between devices: 131 us -> 154 us  [shards(): lax.psum_scatter(lax.dot_general(features, cotangents, (((0,), (0,)), (()...]
    all_to_all x0 -> x1, starting transfers between devices: none -> 11 us  [shards(): lax.all_to_all(jnp.stack([global_params] * lax.axis_size('worker')), 'wor...]
  transfers between devices with their start and end apart: 4 -> 4, of which waited for: 4 -> 3; matrix products, arithmetic and copies ran while one was open for 3% -> 2% of each run, Pallas kernels for 0% -> 0%
where the time goes in v2:
time: 487 us; the launch traced here: 485 us
  waiting for transfers between devices  434 us (89%)
  between operations  15.5 us (3%)
  starting transfers between devices  11.2 us (2%)
  matrix products  10.5 us (2%)
  other arithmetic  10.5 us (2%)
    psum x1, waiting for transfers between devices, shards(): outer_grad = lax.psum(pseudo_grad, 'worker') / replicas  203 us
    reduce_scatter x1, waiting for transfers between devices, shards(): lax.psum_scatter(lax.dot_general(features, cotangents, (((0,), (0,)), (()...  154 us
    all_to_all x1, waiting for transfers between devices, shards(): lax.all_to_all(jnp.stack([global_params] * lax.axis_size('worker')), 'wor...  76.6 us
    all_to_all x1, starting transfers between devices, shards(): lax.all_to_all(jnp.stack([global_params] * lax.axis_size('worker')), 'wor...  11 us
    dot_general x1, matrix products, shards(): lax.dot_general(features, cotangents, (((0,), (0,)), ((), ())), preferred...  10.5 us
  transfers between devices with their start and end apart: 4, of which 3 were waited for; matrix products, arithmetic and copies ran while one was open for 2% of the time, Pallas kernels for 0%

profile of v2, /device:TPU:24, one launch (start us, length us, event | category | flops | bytes accessed | tf_op | source)
XLA Modules:
  0.0 485.4 jit_solution(7887383360606608684)
XLA Ops:
  8.0 0.0 copy-start
  8.0 0.0 reduce-scatter.2.cloned.1.call-start
  8.1 1.0 copy-done
  9.0 10.5 %convolution_convert_fusion = bf16[8192,1024]{1,0:T(8,128)(2,1)} fusion(bf16[1,256,8192]{2,1,0:T(8,128)(2,1)} %param.7, bf16[1,256,1024]{2,1,0:T(8,128)(2,1)S(1)} %copy-done), kind=kOutput, calls=%fused_computation | convolution fusion | flops 4303355904 | bytes 21495808 | tf_op jit(solution)/shard_map/dot_general | solution.py:23
  19.5 0.0 copy-start.1
  19.5 0.0 reduce-scatter.2.cloned.1.call-update
  19.5 0.9 copy-done.1
  20.4 1.6 stack.2
  22.0 11.0 %all-to-all-start = ((f32[16,32,1024]{2,1,0:T(8,128)}), f32[16,32,1024]{2,1,0:T(8,128)S(1)}, u32[]{:S(2)}, u32[]{:S(2)}) async-start(f32[16,32,1024]{2,1,0:T(8,128)} %stack.2), calls=%async_computation | async-start | bytes 4194304 | tf_op jit(solution)/shard_map/all_to_all | solution.py:41
  33.0 0.0 all-gather.2.cloned.1.call-start
  33.1 0.5 all-gather.2.cloned.1.call-update
  33.6 0.0 all-reduce.2.cloned.1.call-start
  33.7 76.6 %all-to-all-done = f32[16,32,1024]{2,1,0:T(8,128)S(1)} async-done(((f32[16,32,1024]{2,1,0:T(8,128)}), f32[16,32,1024]{2,1,0:T(8,128)S(1)}, u32[]{:S(2)}, u32[]{:S(2)}) %all-to-all-start) | async-done | bytes 2097184 | tf_op jit(solution)/shard_map/all_to_all | solution.py:41
  110.3 153.8 %reduce-scatter.2.cloned.1.call-done = bf16[512,1024]{1,0:T(8,128)(2,1)} async-done(((bf16[8192,1024]{1,0:T(8,128)(2,1)}), bf16[512,1024]{1,0:T(8,128)(2,1)}) %reduce-scatter.2.cloned.1.call-update) | async-done | bytes 1048592 | tf_op jit(solution)/shard_map/reduce_scatter | solution.py:22
  264.1 6.2 %fusion.7 = f32[512,1024]{1,0:T(8,128)} fusion(bf16[512,1024]{1,0:T(8,128)(2,1)} %reduce-scatter.2.cloned.1.call-done, f32[1,512,1024]{2,1,0:T(8,128)} %param.9, f32[16,32,1024]{2,1,0:T(8,128)S(1)} %all-to-all-done, f32[1,512,1024]{2,1,0:T(8,128)} %param.11, f32[1,512,1024]{2,1,0:T(8,128)} %param.10), kind=kLoop, calls=%fused_computation.10 | loop fusion | flops 8912896 | bytes 11534336 | tf_op jit(solution)/shard_map/sub | solution.py:46
  270.3 0.0 all-reduce.2.cloned.1.call-update
  270.3 0.0 all-gather.2.cloned.1.call-done
  270.4 202.6 %all-reduce.2.cloned.1.call-done = f32[512,1024]{1,0:T(8,128)} async-done(((f32[512,1024]{1,0:T(8,128)}), f32[512,1024]{1,0:T(8,128)}) %all-reduce.2.cloned.1.call-update) | async-done | bytes 2097168 | tf_op jit(solution)/shard_map/psum | solution.py:47
  472.9 4.3 multiply_add_fusion
  477.3 0.7 constant_dynamic-slice_fusion
Async XLA Ops:
  8.0 1.0 copy-start
  8.0 256.0 %reduce-scatter.2.cloned.1.call-start = ((), (), s32[]{:S(2)}) async-start(), calls=%async_computation.2 | async-start | bytes 17825792 | tf_op jit(solution)/shard_map/reduce_scatter | solution.py:22
  19.5 0.9 copy-start.1
  22.0 88.3 %all-to-all-start = ((f32[16,32,1024]{2,1,0:T(8,128)}), f32[16,32,1024]{2,1,0:T(8,128)S(1)}, u32[]{:S(2)}, u32[]{:S(2)}) async-start(f32[16,32,1024]{2,1,0:T(8,128)} %stack.2), calls=%async_computation | async-start | bytes 4194304 | tf_op jit(solution)/shard_map/all_to_all | solution.py:41
  33.0 237.3 %all-gather.2.cloned.1.call-start = ((), (), s32[]{:S(2)}) async-start(), calls=%async_computation.4 | async-start | bytes 2228224 | tf_op jit(solution)/shard_map/all_gather | solution.py:44
  33.6 439.3 %all-reduce.2.cloned.1.call-start = ((), (), s32[]{:S(2)}) async-start(), calls=%async_computation.3 | async-start | bytes 4194304 | tf_op jit(solution)/shard_map/psum | solution.py:47
Sparse Core Ops, SparseCore 0:
  19.7 244.3 reduce-scatter.1
Sparse Core Ops, SparseCore 1:
  36.2 105.1 all-gather.1
  270.4 202.5 all-reduce.1
